TPU v7x, 32 devices: a whole 2x2x4 slice. The times are simulated.
32 devices in a mesh: sec: 4 (over y, x), dom: 8 (over z, core).
Axes of the slice: x: 2, y: 2, z: 4, core: 2. Of those that a mesh axis runs over, the one named last changes fastest.
Arguments:
- state_init: float32 [4, 8, 6, 1536], P('sec', 'dom'), may hold values from -6 to 6
- right_side: float32 [4, 8, 6, 1536], P('sec', 'dom'), may hold values from -6 to 6
- diag_inverse: float32 [4, 8, 6, 6, 1536], P('sec', 'dom'), may hold values from -1.2 to 2, as said below
- face_block: bfloat16 [4, 8, 6, 6, 9216], P('sec', 'dom'), may hold values from -0.47851562 to 0.47851562
- face_target: int32 [4, 8, 9216], P('sec', 'dom'), may hold values from 0 to 1535
- face_source: int32 [4, 8, 9216], P('sec', 'dom'), may hold values from 0 to 3071, as said below
- face_count: int32 [4, 8], P('sec', 'dom'), may hold values from 4608 to 9216, as said below
- send_list: int32 [4, 8, 1536], P('sec', 'dom'), may hold values from 0 to 1535
- surf_cell: int32 [4, 8, 128], P('sec', 'dom'), may hold values from 0 to 1535
- surf_count: int32 [4, 8, 8], P('sec', 'dom'), may hold values from 0 to 16, as said below
- surf_map: float32 [4, 8, 3, 6, 128], P('sec', 'dom'), may hold values from -3 to 3
- surf_node: int32 [3, 8, 128], P(None, 'dom'), may hold values from 0 to 1535
Outputs:
- state_final: float32 [4, 8, 6, 1536], P('sec', 'dom')
Inputs may be any that keep to these rules, and one draw needn't show every extreme that they name: `face_source`: values below 1536 name the partition's own cells; a value 1536 + r * 192 + k names slot k of neighbour block r, which comes from partition d - offset r of the same section; only existing partitions are read, and each block is read in a leading run of its slots whose length differs from block to block; some block's run is 192 long. Only the first face_count entries of a partition's face lists are live; some partition lists 9216 live entries. Live slots of a flow partition towards structure partition o are its first surf_count slots of that block. Only some flow partitions (those at the wall, drawn from the seed) have live slots, each towards a few structure partitions of consecutive index (mod 8); some pair has 16 live slots. The structure section's row is zero and not read. `diag_inverse`: each block is a transposed block inverse; its diagonal entries are positive.
All inputs are finite; a program needn't handle non-finite values.
Results may differ from a plain program's by a relative error of at most 0.0003.
Values sent between devices are 32-bit elements; how exact they have to be, the bound alone decides.
A program may use at most 128 MiB of HBM per device.

v0:
```python
import jax
import jax.numpy as jnp
from jax import lax
from jax.sharding import PartitionSpec as P

NVAR = 6
NLOAD = 3
NBR = 8
ITERS = 2
neighbour_offsets = (1, -1, 2, -2, 3, -3, 4, -4)


def shifted(value, axis, steps):
    count = lax.axis_size(axis)
    first, last = (max(0, -steps), min(count, count - steps))
    return lax.ppermute(value, axis, [(source, source + steps) for source in range(first, last)])


def apply_blocks(blocks, vector):
    width = blocks.shape[-2]
    total = blocks[..., :, 0, :].astype(jnp.float32) * vector[..., 0:1, :]
    for column in range(1, width):
        total = (
            total
            + blocks[..., :, column, :].astype(jnp.float32) * vector[..., column : column + 1, :]
        )
    return total


def apply_transposed(blocks, vector):
    height = blocks.shape[-3]
    total = blocks[..., 0, :, :] * vector[..., 0:1, :]
    for row_index in range(1, height):
        total = total + blocks[..., row_index, :, :] * vector[..., row_index : row_index + 1, :]
    return total


def body(
    state_init,
    right_side,
    diag_inverse,
    face_block,
    face_target,
    face_source,
    face_count,
    send_list,
    surf_cell,
    surf_count,
    surf_map,
    surf_node,
):
    state = state_init[0, 0]
    source_terms = right_side[0, 0]
    inverse = diag_inverse[0, 0]
    blocks = face_block[0, 0]
    targets = face_target[0, 0]
    sources = face_source[0, 0]
    live_faces = face_count[0, 0]
    outgoing_cells = send_list[0, 0]
    surface_cells = surf_cell[0, 0]
    slot_counts = surf_count[0, 0]
    coupling_map = surf_map[0, 0]
    node_table = surf_node[:, 0]
    cells = state.shape[1]
    faces = blocks.shape[2]
    dom_size = lax.axis_size("dom")
    block_slots = outgoing_cells.shape[0] // NBR
    final_row = lax.axis_size("sec") - 1
    sec_index = lax.axis_index("sec")
    is_structure = sec_index == final_row
    capacity = surface_cells.shape[0] // dom_size
    face_mask = (jnp.arange(faces, dtype=jnp.int32) < live_faces).astype(jnp.float32)
    slot_mask = (
        (jnp.arange(capacity, dtype=jnp.int32)[None, :] < slot_counts[:, None])
        .reshape(-1)
        .astype(jnp.float32)
    )
    slot_mask = slot_mask * jnp.where(is_structure, 0.0, 1.0)
    own_row = jnp.minimum(sec_index, final_row - 1)
    own_nodes = lax.dynamic_index_in_dim(node_table, own_row, 0, keepdims=False)
    for sweep in range(ITERS):
        outgoing = state[:, outgoing_cells]
        pieces = []
        for index in range(NBR):
            block_out = outgoing[:, index * block_slots : (index + 1) * block_slots]
            pieces.append(shifted(block_out, "dom", neighbour_offsets[index]))
        ghosts = jnp.concatenate(pieces, axis=1)
        extended = jnp.concatenate([state, ghosts], axis=1)
        gathered = extended[:, sources]
        contrib = apply_blocks(blocks, gathered) * face_mask[None, :]
        face_terms = jnp.zeros((NVAR, cells), jnp.float32).at[:, targets].add(contrib)
        loads = apply_blocks(coupling_map, state[:, surface_cells]) * slot_mask[None, :]
        arrived = lax.all_to_all(loads, "dom", split_axis=1, concat_axis=1, tiled=True)
        displaced = jnp.where(is_structure, state[:NLOAD], 0.0)
        dense_loads = jnp.zeros((NLOAD, cells), jnp.float32).at[:, own_nodes].add(arrived)
        load_total, column_disp = lax.psum((dense_loads, displaced), "sec")
        looked_up = column_disp[:, own_nodes]
        returned = (
            lax.all_to_all(looked_up, "dom", split_axis=1, concat_axis=1, tiled=True)
            * slot_mask[None, :]
        )
        pushed = apply_transposed(coupling_map, returned)
        flow_coupling = jnp.zeros((NVAR, cells), jnp.float32).at[:, surface_cells].add(pushed)
        struct_coupling = jnp.concatenate(
            [load_total, jnp.zeros((NVAR - NLOAD, cells), jnp.float32)], axis=0
        )
        coupling = jnp.where(is_structure, struct_coupling, flow_coupling)
        state = apply_blocks(inverse, source_terms - face_terms - coupling)
    return state[None, None]


def solution(mesh):
    in_specs = (
        P("sec", "dom", None, None),
        P("sec", "dom", None, None),
        P("sec", "dom", None, None, None),
        P("sec", "dom", None, None, None),
        P("sec", "dom", None),
        P("sec", "dom", None),
        P("sec", "dom"),
        P("sec", "dom", None),
        P("sec", "dom", None),
        P("sec", "dom", None),
        P("sec", "dom", None, None, None),
        P(None, "dom", None),
    )
    out_specs = P("sec", "dom", None, None)
    return jax.shard_map(body, mesh=mesh, in_specs=in_specs, out_specs=out_specs, check_vma=False)
```

profile of v0, /device:TPU:0, one launch (start us, length us, event | category | flops | bytes accessed | tf_op | source)
XLA Modules:
  0.0 484.6 jit_solution(1774488598289809015)
XLA Ops:
  0.0 1.1 copy.140
  1.8 2.6 gather_fusion
  4.4 0.9 fusion.56
  5.4 3.1 collective-permute-start
  8.5 1.3 collective-permute-start.1
  9.8 6.9 %collective-permute-start.2 = (f32[6,192]{0,1:T(8,128)}, f32[6,192]{0,1:T(8,128)}, u32[]{:S(2)}, u32[]{:S(2)}) collective-permute-start(f32[6,192]{0,1:T(8,128)} %get-tuple-element.72), channel_id=1, source_target_pairs={{0,2},{1,3},{2,4},{3,5},{4,6},{5,7},{8,10},{9,11},{10,12},{11,13},... | collective-permute-start | bytes 13832 | tf_op jit(solution)/shard_map/ppermute | solution.py:16
  16.7 1.3 collective-permute-start.3
  17.9 4.2 collective-permute-start.4
  24.9 4.0 all-to-all-start
  30.3 5.4 %fusion.54 = (bf16[6,1,9216]{2,1,0:T(2,128)(2,1)S(1)}, bf16[6,1,9216]{2,1,0:T(2,128)(2,1)S(1)}, bf16[6,1,9216]{2,1,0:T(2,128)(2,1)S(1)}, bf16[6,1,9216]{2,1,0:T(...) fusion(bf16[6,6,9216]{2,1,0:T(8,128)(2,1)} %bitcast.228), kind=kLoop, calls=%fused_computation.187 | loop fusion | flops 55296 | bytes 1437696 | tf_op jit(solution)/shard_map/slice | solution.py:25
  38.0 1.0 select_bitcast_fusion
  39.7 3.3 copy.137
  44.3 1.9 scatter_custom_fusion.1
  46.2 60.9 %all-reduce.3 = (f32[3,1536]{0,1:T(8,128)}, f32[3,1536]{0,1:T(8,128)}) all-reduce(f32[3,1536]{0,1:T(8,128)} %select_bitcast_fusion, f32[3,1536]{0,1:T(8,128)} %scatter_custom_fusion.1), channel_id=1, replica_groups=mesh['sec'=4,'dom'=8] {'sec'}, use_global_device_ids=true, to_apply=%region_3.4 | all-reduce | flops 9216 | bytes 73728 | tf_op jit(solution)/shard_map/psum | solution.py:96
  107.1 1.8 gather_fusion.3
  109.6 3.9 all-to-all-start.1
  113.5 1.3 collective-permute-start.5
  114.8 0.9 constant_dynamic-update-slice_fusion.7
  115.7 5.4 %collective-permute-start.6 = (f32[6,192]{0,1:T(8,128)S(1)}, f32[6,192]{0,1:T(8,128)S(1)}, u32[]{:S(2)}, u32[]{:S(2)}) collective-permute-start(f32[6,192]{0,1:T(8,128)S(1)} %copy-done.24), channel_id=1, source_target_pairs={{0,4},{1,5},{2,6},{3,7},{8,12},{9,13},{10,14},{11,15},{16,20},{17,... | collective-permute-start | bytes 13832 | tf_op jit(solution)/shard_map/ppermute | solution.py:16
  121.1 0.9 constant_dynamic-update-slice_fusion.6
  122.1 1.5 collective-permute-start.7
  123.5 0.9 constant_dynamic-update-slice_fusion.5
  124.5 0.9 constant_dynamic-update-slice_fusion.4
  125.4 0.9 constant_dynamic-update-slice_fusion.3
  126.3 5.9 %collective-permute-done.7 = f32[6,192]{0,1:T(8,128)S(1)} collective-permute-done((f32[6,192]{0,1:T(8,128)S(1)}, f32[6,192]{0,1:T(8,128)S(1)}, u32[]{:S(2)}, u32[]{:S(2)}) %collective-permute-start.7) | collective-permute-done | bytes 4640 | tf_op jit(solution)/shard_map/ppermute | solution.py:16
  132.3 31.0 %gather_fusion.1 = f32[9216,6]{1,0:T(8,128)} fusion(f32[6,3072]{0,1:T(8,128)S(1)} %constant_dynamic-update-slice_fusion, s32[9216]{0:T(1024)S(1)} %copy-done.8), kind=kCustom, calls=%fused_computation.1 | custom fusion | bytes 479232 | tf_op jit(solution)/shard_map/gather | solution.py:89
  163.2 23.4 %slice_reduce_fusion.11 = (f32[9216]{0:T(1024)S(1)}, f32[9216]{0:T(1024)S(1)}, f32[9216]{0:T(1024)S(1)}, f32[9216]{0:T(1024)S(1)}, f32[9216]{0:T(1024)S(1)}, /*index=5*/f32[9216]{0:T(1024)S(1)}) fusion(f32[6,9216]{0,1:T(8,128)} %bitcast.217), kind=kLoop, calls=%fused_computation.25 | loop fusion | bytes 442368 | tf_op jit(solution)/shard_map/slice | solution.py:21
  187.1 2.9 copy.145
  190.1 49.9 %scatter_custom_fusion = f32[6,1536]{0,1:T(8,128)S(1)} fusion(s32[9216]{0:T(1024)} %bitcast.235, f32[9216,6]{1,0:T(8,128)} %copy.145, f32[]{:T(128)} %constant.8.clone.1), kind=kCustom, calls=%fused_computation.76 | custom fusion | flops 55296 | bytes 37376 | tf_op jit(solution)/shard_map/scatter-add | solution.py:91
  241.6 1.7 scatter_custom_fusion.2
  243.4 1.4 fusion.10
  244.8 2.3 slice_reduce_fusion.23
  247.1 2.6 constant_dynamic-update-slice_fusion.17
  249.8 4.9 %gather_fusion.4 = f32[1536,6]{1,0:T(8,128)} fusion(f32[6,1536]{0,1:T(8,128)} %get-tuple-element.52, s32[2048]{0:T(1024)S(1)} %pad_clamp_fusion), kind=kCustom, calls=%fused_computation.4 | custom fusion | bytes 79872 | tf_op jit(solution)/shard_map/gather | solution.py:82
  254.7 2.1 slice_select_fusion
  256.7 1.9 gather_fusion.6
  260.1 3.3 all-to-all-start.2
  263.5 2.0 fusion.55
  265.5 2.9 collective-permute-start.8
  268.4 1.3 collective-permute-start.9
  269.7 5.8 %collective-permute-start.10 = (f32[6,192]{0,1:T(8,128)}, f32[6,192]{0,1:T(8,128)}, u32[]{:S(2)}, u32[]{:S(2)}) collective-permute-start(f32[6,192]{0,1:T(8,128)} %get-tuple-element.64), channel_id=1, source_target_pairs={{0,2},{1,3},{2,4},{3,5},{4,6},{5,7},{8,10},{9,11},{10,12},{11,13},... | collective-permute-start | bytes 13832 | tf_op jit(solution)/shard_map/ppermute | solution.py:16
  275.5 1.3 collective-permute-start.11
  276.8 4.1 collective-permute-start.12
  281.1 2.0 scatter_custom_fusion.4
  283.1 59.9 %all-reduce.2 = (f32[3,1536]{0,1:T(8,128)}, f32[3,1536]{0,1:T(8,128)}) all-reduce(f32[3,1536]{0,1:T(8,128)} %slice_select_fusion, f32[3,1536]{0,1:T(8,128)} %scatter_custom_fusion.4), channel_id=1, replica_groups=mesh['sec'=4,'dom'=8] {'sec'}, use_global_device_ids=true, to_apply=%region_8.9 | all-reduce | flops 9216 | bytes 73728 | tf_op jit(solution)/shard_map/psum | solution.py:96
  343.0 1.9 gather_fusion.7
  345.6 3.9 all-to-all-start.3
  349.5 1.3 collective-permute-start.13
  350.8 0.9 constant_dynamic-update-slice_fusion.16
  351.7 5.4 %collective-permute-start.14 = (f32[6,192]{0,1:T(8,128)S(1)}, f32[6,192]{0,1:T(8,128)S(1)}, u32[]{:S(2)}, u32[]{:S(2)}) collective-permute-start(f32[6,192]{0,1:T(8,128)S(1)} %get-tuple-element.60), channel_id=1, source_target_pairs={{0,4},{1,5},{2,6},{3,7},{8,12},{9,13},{10,14},{11,15},{16,20},{17,... | collective-permute-start | bytes 13832 | tf_op jit(solution)/shard_map/ppermute | solution.py:16
  357.1 0.9 constant_dynamic-update-slice_fusion.15
  358.0 1.6 collective-permute-start.15
  359.6 0.9 constant_dynamic-update-slice_fusion.14
  360.5 0.9 constant_dynamic-update-slice_fusion.13
  361.4 0.9 constant_dynamic-update-slice_fusion.12
  362.3 5.6 %collective-permute-done.15 = f32[6,192]{0,1:T(8,128)S(1)} collective-permute-done((f32[6,192]{0,1:T(8,128)S(1)}, f32[6,192]{0,1:T(8,128)S(1)}, u32[]{:S(2)}, u32[]{:S(2)}) %collective-permute-start.15) | collective-permute-done | bytes 4640 | tf_op jit(solution)/shard_map/ppermute | solution.py:16
  367.9 31.0 %gather_fusion.5 = f32[9216,6]{1,0:T(8,128)} fusion(f32[6,3072]{0,1:T(8,128)S(1)} %constant_dynamic-update-slice_fusion.9, s32[9216]{0:T(1024)S(1)} %copy-done.9), kind=kCustom, calls=%fused_computation.5 | custom fusion | bytes 479232 | tf_op jit(solution)/shard_map/gather | solution.py:89
  398.9 23.4 %slice_reduce_fusion.5 = (f32[9216]{0:T(1024)S(1)}, f32[9216]{0:T(1024)S(1)}, f32[9216]{0:T(1024)S(1)}, f32[9216]{0:T(1024)S(1)}, f32[9216]{0:T(1024)S(1)}, /*index=5*/f32[9216]{0:T(1024)S(1)}) fusion(f32[6,9216]{0,1:T(8,128)} %bitcast.216), kind=kLoop, calls=%fused_computation.19 | loop fusion | bytes 442368 | tf_op jit(solution)/shard_map/slice | solution.py:21
  422.8 2.9 copy.155
  425.7 49.9 %scatter_custom_fusion.3 = f32[6,1536]{0,1:T(8,128)S(1)} fusion(s32[9216]{0:T(1024)} %bitcast.236, f32[9216,6]{1,0:T(8,128)} %copy.155, f32[]{:T(128)} %constant.8.clone.1), kind=kCustom, calls=%fused_computation.72 | custom fusion | flops 55296 | bytes 37376 | tf_op jit(solution)/shard_map/scatter-add | solution.py:91
  476.6 1.6 scatter_custom_fusion.5
  478.3 1.4 fusion.11
  479.7 2.3 slice_reduce_fusion.17
  482.1 1.7 fusion
  (194 shorter events, 15.7 us)
Async XLA Ops:
  0.0 22.1 %copy-start.45 = (s32[1,1,128]{2,1,0:T(1,128)S(1)}, s32[1,1,128]{2,1,0:T(1,128)}, u32[]{:S(2)}) copy-start(s32[1,1,128]{2,1,0:T(1,128)} %param.20) | copy-start | bytes 1540
  0.0 22.1 %copy-start.31 = (f32[1,1,3,6,128]{4,1,3,2,0:T(1,128)S(1)}, f32[1,1,3,6,128]{4,1,3,2,0:T(1,128)}, u32[]{:S(2)}) copy-start(f32[1,1,3,6,128]{4,1,3,2,0:T(1,128)} %param.22) | copy-start | bytes 27652
  0.0 24.1 %copy-start.42 = (s32[1,1,8]{2,1,0:T(1,128)S(1)}, s32[1,1,8]{2,1,0:T(1,128)}, u32[]{:S(2)}) copy-start(s32[1,1,8]{2,1,0:T(1,128)} %param.21) | copy-start | bytes 100
  5.4 24.2 %copy-start.29 = (s32[1,1,9216]{2,1,0:T(1,128)S(1)}, s32[1,1,9216]{2,1,0:T(1,128)}, u32[]{:S(2)}) copy-start(s32[1,1,9216]{2,1,0:T(1,128)} %param.16) | copy-start | bytes 110596
  5.4 108.1 %collective-permute-start = (f32[6,192]{0,1:T(8,128)}, f32[6,192]{0,1:T(8,128)}, u32[]{:S(2)}, u32[]{:S(2)}) collective-permute-start(f32[6,192]{0,1:T(8,128)} %get-tuple-element.74), channel_id=1, source_target_pairs={{0,1},{1,2},{2,3},{3,4},{4,5},{5,6},{6,7},{8,9},{9,10},{10,11},{11... | collective-permute-start | bytes 13832 | tf_op jit(solution)/shard_map/ppermute | solution.py:16
  8.5 107.2 %collective-permute-start.1 = (f32[6,192]{0,1:T(8,128)}, f32[6,192]{0,1:T(8,128)}, u32[]{:S(2)}, u32[]{:S(2)}) collective-permute-start(f32[6,192]{0,1:T(8,128)} %get-tuple-element.73), channel_id=1, source_target_pairs={{1,0},{2,1},{3,2},{4,3},{5,4},{6,5},{7,6},{9,8},{10,9},{11,10},{12... | collective-permute-start | bytes 13832 | tf_op jit(solution)/shard_map/ppermute | solution.py:16
  9.8 112.3 %collective-permute-start.2 = (f32[6,192]{0,1:T(8,128)}, f32[6,192]{0,1:T(8,128)}, u32[]{:S(2)}, u32[]{:S(2)}) collective-permute-start(f32[6,192]{0,1:T(8,128)} %get-tuple-element.72), channel_id=1, source_target_pairs={{0,2},{1,3},{2,4},{3,5},{4,6},{5,7},{8,10},{9,11},{10,12},{11,13},... | collective-permute-start | bytes 13832 | tf_op jit(solution)/shard_map/ppermute | solution.py:16
  16.7 107.8 %collective-permute-start.3 = (f32[6,192]{0,1:T(8,128)}, f32[6,192]{0,1:T(8,128)}, u32[]{:S(2)}, u32[]{:S(2)}) collective-permute-start(f32[6,192]{0,1:T(8,128)} %get-tuple-element.71), channel_id=1, source_target_pairs={{2,0},{3,1},{4,2},{5,3},{6,4},{7,5},{10,8},{11,9},{12,10},{13,11},... | collective-permute-start | bytes 13832 | tf_op jit(solution)/shard_map/ppermute | solution.py:16
  17.9 107.4 %collective-permute-start.4 = (f32[6,192]{0,1:T(8,128)}, f32[6,192]{0,1:T(8,128)}, u32[]{:S(2)}, u32[]{:S(2)}) collective-permute-start(f32[6,192]{0,1:T(8,128)} %get-tuple-element.70), channel_id=1, source_target_pairs={{0,3},{1,4},{2,5},{3,6},{4,7},{8,11},{9,12},{10,13},{11,14},{12,15... | collective-permute-start | bytes 13832 | tf_op jit(solution)/shard_map/ppermute | solution.py:16
  22.3 8.0 %copy-start.11 = (f32[3,8,16]{2,1,0:T(8,128)}, f32[3,8,16]{2,1,0:T(8,128)S(1)}, u32[]{:S(2)}) copy-start(f32[3,8,16]{2,1,0:T(8,128)S(1)} %squeeze.137) | copy-start | bytes 4612
  22.4 7.9 %copy-start.13 = (f32[3,8,16]{2,1,0:T(8,128)}, f32[3,8,16]{2,1,0:T(8,128)S(1)}, u32[]{:S(2)}) copy-start(f32[3,8,16]{2,1,0:T(8,128)S(1)} %squeeze.136) | copy-start | bytes 4612
  22.4 7.8 %copy-start.15 = (f32[3,8,16]{2,1,0:T(8,128)}, f32[3,8,16]{2,1,0:T(8,128)S(1)}, u32[]{:S(2)}) copy-start(f32[3,8,16]{2,1,0:T(8,128)S(1)} %squeeze.135) | copy-start | bytes 4612
  22.5 7.7 %copy-start.17 = (f32[3,8,16]{2,1,0:T(8,128)}, f32[3,8,16]{2,1,0:T(8,128)S(1)}, u32[]{:S(2)}) copy-start(f32[3,8,16]{2,1,0:T(8,128)S(1)} %squeeze.134) | copy-start | bytes 4612
  22.6 7.6 %copy-start.19 = (f32[3,8,16]{2,1,0:T(8,128)}, f32[3,8,16]{2,1,0:T(8,128)S(1)}, u32[]{:S(2)}) copy-start(f32[3,8,16]{2,1,0:T(8,128)S(1)} %squeeze.133) | copy-start | bytes 4612
  22.7 7.6 %copy-start.21 = (f32[3,8,16]{2,1,0:T(8,128)}, f32[3,8,16]{2,1,0:T(8,128)S(1)}, u32[]{:S(2)}) copy-start(f32[3,8,16]{2,1,0:T(8,128)S(1)} %squeeze.131) | copy-start | bytes 4612
  22.7 7.5 %copy-start.38 = (s32[1024]{0:T(1024)}, s32[1024]{0:T(1024)S(1)}, u32[]{:S(2)}) copy-start(s32[1024]{0:T(1024)S(1)} %pad_clamp_fusion.2) | copy-start | bytes 12292
  24.2 15.4 %copy-start.26 = (f32[8,16]{1,0:T(8,128)}, f32[8,16]{1,0:T(8,128)S(1)}, u32[]{:S(2)}) copy-start(f32[8,16]{1,0:T(8,128)S(1)} %fusion.50) | copy-start | bytes 1540
  24.9 18.5 %all-to-all-start = ((f32[3,8,16]{2,0,1:T(4,128)}), f32[3,8,16]{2,0,1:T(4,128)}, u32[]{:S(2)}, u32[]{:S(2)}) async-start(f32[3,8,16]{2,0,1:T(4,128)} %copy.146), calls=%async_computation | async-start | bytes 32768 | tf_op jit(solution)/shard_map/all_to_all | solution.py:93
  28.9 8.1 %copy-start.30 = (s32[1,1,9216]{2,1,0:T(1,128)S(1)}, s32[1,1,9216]{2,1,0:T(1,128)}, u32[]{:S(2)}) copy-start(s32[1,1,9216]{2,1,0:T(1,128)} %param.17) | copy-start | bytes 110596
  28.9 8.7 %slice-start.4 = ((f32[1,1,6,1536]{3,1,2,0:T(1,128)}), f32[1,1,3,1536]{3,1,2,0:T(1,128)S(1)}, s32[]{:S(2)}) async-start(f32[1,1,6,1536]{3,1,2,0:T(1,128)} %param.12), calls=%async_computation.8 | async-start | bytes 36864 | tf_op jit(solution)/shard_map/slice | solution.py:94
  39.6 67.5 %copy-start.39 = (s32[1024]{0:T(1024)}, s32[1024]{0:T(1024)S(1)}, u32[]{:S(2)}) copy-start(s32[1024]{0:T(1024)S(1)} %pad_clamp_fusion.1) | copy-start | bytes 12292
  39.7 201.1 %copy-start.40 = (f32[128]{0:T(128)}, f32[128]{0:T(128)S(1)}, u32[]{:S(2)}) copy-start(f32[128]{0:T(128)S(1)} %mul.568) | copy-start | bytes 1540
  43.1 70.4 %copy-start.25 = (f32[6,192]{0,1:T(8,128)S(1)}, f32[6,192]{0,1:T(8,128)}, u32[]{:S(2)}) copy-start(f32[6,192]{0,1:T(8,128)} %get-tuple-element.69) | copy-start | bytes 13828
  43.4 72.4 %copy-start.24 = (f32[6,192]{0,1:T(8,128)S(1)}, f32[6,192]{0,1:T(8,128)}, u32[]{:S(2)}) copy-start(f32[6,192]{0,1:T(8,128)} %get-tuple-element.68) | copy-start | bytes 13828
  43.4 78.7 %copy-start.23 = (f32[6,192]{0,1:T(8,128)S(1)}, f32[6,192]{0,1:T(8,128)}, u32[]{:S(2)}) copy-start(f32[6,192]{0,1:T(8,128)} %get-tuple-element.67) | copy-start | bytes 13828
  46.2 86.0 %copy-start.8 = (s32[9216]{0:T(1024)S(1)}, s32[9216]{0:T(1024)}, u32[]{:S(2)}) copy-start(s32[9216]{0:T(1024)} %broadcast_clamp_fusion) | copy-start | bytes 110596
  109.6 130.4 %all-to-all-start.1 = ((f32[3,8,16]{2,0,1:T(4,128)}), f32[3,8,16]{2,0,1:T(4,128)}, u32[]{:S(2)}, u32[]{:S(2)}) async-start(f32[3,8,16]{2,0,1:T(4,128)} %copy.150), calls=%async_computation.1 | async-start | bytes 32768 | tf_op jit(solution)/shard_map/all_to_all | solution.py:99
  113.5 12.8 %collective-permute-start.5 = (f32[6,192]{0,1:T(8,128)S(1)}, f32[6,192]{0,1:T(8,128)S(1)}, u32[]{:S(2)}, u32[]{:S(2)}) collective-permute-start(f32[6,192]{0,1:T(8,128)S(1)} %copy-done.25), channel_id=1, source_target_pairs={{3,0},{4,1},{5,2},{6,3},{7,4},{11,8},{12,9},{13,10},{14,11},{15,12... | collective-permute-start | bytes 13832 | tf_op jit(solution)/shard_map/ppermute | solution.py:16
  115.7 10.6 %collective-permute-start.6 = (f32[6,192]{0,1:T(8,128)S(1)}, f32[6,192]{0,1:T(8,128)S(1)}, u32[]{:S(2)}, u32[]{:S(2)}) collective-permute-start(f32[6,192]{0,1:T(8,128)S(1)} %copy-done.24), channel_id=1, source_target_pairs={{0,4},{1,5},{2,6},{3,7},{8,12},{9,13},{10,14},{11,15},{16,20},{17,... | collective-permute-start | bytes 13832 | tf_op jit(solution)/shard_map/ppermute | solution.py:16
  122.1 10.2 %collective-permute-start.7 = (f32[6,192]{0,1:T(8,128)S(1)}, f32[6,192]{0,1:T(8,128)S(1)}, u32[]{:S(2)}, u32[]{:S(2)}) collective-permute-start(f32[6,192]{0,1:T(8,128)S(1)} %copy-done.23), channel_id=1, source_target_pairs={{4,0},{5,1},{6,2},{7,3},{12,8},{13,9},{14,10},{15,11},{20,16},{21,... | collective-permute-start | bytes 13832 | tf_op jit(solution)/shard_map/ppermute | solution.py:16
  163.2 23.5 %copy-start = (bf16[6,1,9216]{2,1,0:T(2,128)(2,1)S(1)}, bf16[6,1,9216]{2,1,0:T(2,128)(2,1)}, u32[]{:S(2)}) copy-start(bf16[6,1,9216]{2,1,0:T(2,128)(2,1)} %get-tuple-element.56) | copy-start | bytes 331780
  163.2 23.5 %copy-start.2 = (bf16[6,1,9216]{2,1,0:T(2,128)(2,1)S(1)}, bf16[6,1,9216]{2,1,0:T(2,128)(2,1)}, u32[]{:S(2)}) copy-start(bf16[6,1,9216]{2,1,0:T(2,128)(2,1)} %get-tuple-element.57) | copy-start | bytes 331780
  163.2 23.5 %copy-start.4 = (f32[6,1,9216]{2,1,0:T(1,128)S(1)}, f32[6,1,9216]{2,1,0:T(1,128)}, u32[]{:S(2)}) copy-start(f32[6,1,9216]{2,1,0:T(1,128)} %get-tuple-element.58) | copy-start | bytes 663556
  163.2 23.5 %copy-start.6 = (f32[9216]{0:T(1024)S(1)}, f32[9216]{0:T(1024)}, u32[]{:S(2)}) copy-start(f32[9216]{0:T(1024)} %fusion.38) | copy-start | bytes 110596
  187.1 53.7 %copy-start.32 = (f32[1,1,1,6,128]{4,1,3,2,0:T(1,128)S(1)}, f32[1,1,1,6,128]{4,1,3,2,0:T(1,128)}, u32[]{:S(2)}) copy-start(f32[1,1,1,6,128]{4,1,3,2,0:T(1,128)} %get-tuple-element.75) | copy-start | bytes 9220
  187.1 53.7 %copy-start.34 = (f32[1,1,1,6,128]{4,1,3,2,0:T(1,128)S(1)}, f32[1,1,1,6,128]{4,1,3,2,0:T(1,128)}, u32[]{:S(2)}) copy-start(f32[1,1,1,6,128]{4,1,3,2,0:T(1,128)} %get-tuple-element.76) | copy-start | bytes 9220
  187.1 53.7 %copy-start.36 = (f32[1,1,1,6,128]{4,1,3,2,0:T(1,128)S(1)}, f32[1,1,1,6,128]{4,1,3,2,0:T(1,128)}, u32[]{:S(2)}) copy-start(f32[1,1,1,6,128]{4,1,3,2,0:T(1,128)} %get-tuple-element.77) | copy-start | bytes 9220
  240.9 6.2 %slice-start = ((s8[4718592]{0:T(1024)(128)(4,1)}), s8[524288]{0:T(1024)(128)(4,1)S(1)}, s32[]{:S(2)}) async-start(s8[4718592]{0:T(1024)(128)(4,1)} %bitcast.218), calls=%async_computation.4 | async-start | bytes 1048576
  249.7 9.7 %copy-start.12 = (f32[3,8,16]{2,1,0:T(8,128)S(1)}, f32[3,8,16]{2,1,0:T(8,128)}, u32[]{:S(2)}) copy-start(f32[3,8,16]{2,1,0:T(8,128)} %copy-done.11) | copy-start | bytes 4612
  249.7 9.7 %copy-start.14 = (f32[3,8,16]{2,1,0:T(8,128)S(1)}, f32[3,8,16]{2,1,0:T(8,128)}, u32[]{:S(2)}) copy-start(f32[3,8,16]{2,1,0:T(8,128)} %copy-done.13) | copy-start | bytes 4612
  249.7 9.7 %copy-start.16 = (f32[3,8,16]{2,1,0:T(8,128)S(1)}, f32[3,8,16]{2,1,0:T(8,128)}, u32[]{:S(2)}) copy-start(f32[3,8,16]{2,1,0:T(8,128)} %copy-done.15) | copy-start | bytes 4612
  249.8 9.7 %copy-start.18 = (f32[3,8,16]{2,1,0:T(8,128)S(1)}, f32[3,8,16]{2,1,0:T(8,128)}, u32[]{:S(2)}) copy-start(f32[3,8,16]{2,1,0:T(8,128)} %copy-done.17) | copy-start | bytes 4612
  249.8 9.7 %copy-start.20 = (f32[3,8,16]{2,1,0:T(8,128)S(1)}, f32[3,8,16]{2,1,0:T(8,128)}, u32[]{:S(2)}) copy-start(f32[3,8,16]{2,1,0:T(8,128)} %copy-done.19) | copy-start | bytes 4612
  249.8 9.7 %copy-start.22 = (f32[3,8,16]{2,1,0:T(8,128)S(1)}, f32[3,8,16]{2,1,0:T(8,128)}, u32[]{:S(2)}) copy-start(f32[3,8,16]{2,1,0:T(8,128)} %copy-done.21) | copy-start | bytes 4612
  249.8 9.7 %copy-start.27 = (f32[8,16]{1,0:T(8,128)S(1)}, f32[8,16]{1,0:T(8,128)}, u32[]{:S(2)}) copy-start(f32[8,16]{1,0:T(8,128)} %copy-done.26) | copy-start | bytes 1540
  260.1 20.8 %all-to-all-start.2 = ((f32[3,8,16]{2,0,1:T(4,128)}), f32[3,8,16]{2,0,1:T(4,128)S(1)}, u32[]{:S(2)}, u32[]{:S(2)}) async-start(f32[3,8,16]{2,0,1:T(4,128)} %copy.156), calls=%async_computation.2 | async-start | bytes 32768 | tf_op jit(solution)/shard_map/all_to_all | solution.py:93
  265.5 84.0 %collective-permute-start.8 = (f32[6,192]{0,1:T(8,128)}, f32[6,192]{0,1:T(8,128)}, u32[]{:S(2)}, u32[]{:S(2)}) collective-permute-start(f32[6,192]{0,1:T(8,128)} %get-tuple-element.66), channel_id=1, source_target_pairs={{0,1},{1,2},{2,3},{3,4},{4,5},{5,6},{6,7},{8,9},{9,10},{10,11},{11... | collective-permute-start | bytes 13832 | tf_op jit(solution)/shard_map/ppermute | solution.py:16
  268.4 83.3 %collective-permute-start.9 = (f32[6,192]{0,1:T(8,128)}, f32[6,192]{0,1:T(8,128)}, u32[]{:S(2)}, u32[]{:S(2)}) collective-permute-start(f32[6,192]{0,1:T(8,128)} %get-tuple-element.65), channel_id=1, source_target_pairs={{1,0},{2,1},{3,2},{4,3},{5,4},{6,5},{7,6},{9,8},{10,9},{11,10},{12... | collective-permute-start | bytes 13832 | tf_op jit(solution)/shard_map/ppermute | solution.py:16
  269.7 88.3 %collective-permute-start.10 = (f32[6,192]{0,1:T(8,128)}, f32[6,192]{0,1:T(8,128)}, u32[]{:S(2)}, u32[]{:S(2)}) collective-permute-start(f32[6,192]{0,1:T(8,128)} %get-tuple-element.64), channel_id=1, source_target_pairs={{0,2},{1,3},{2,4},{3,5},{4,6},{5,7},{8,10},{9,11},{10,12},{11,13},... | collective-permute-start | bytes 13832 | tf_op jit(solution)/shard_map/ppermute | solution.py:16
  275.5 85.0 %collective-permute-start.11 = (f32[6,192]{0,1:T(8,128)}, f32[6,192]{0,1:T(8,128)}, u32[]{:S(2)}, u32[]{:S(2)}) collective-permute-start(f32[6,192]{0,1:T(8,128)} %get-tuple-element.63), channel_id=1, source_target_pairs={{2,0},{3,1},{4,2},{5,3},{6,4},{7,5},{10,8},{11,9},{12,10},{13,11},... | collective-permute-start | bytes 13832 | tf_op jit(solution)/shard_map/ppermute | solution.py:16
  276.8 84.6 %collective-permute-start.12 = (f32[6,192]{0,1:T(8,128)S(1)}, f32[6,192]{0,1:T(8,128)}, u32[]{:S(2)}, u32[]{:S(2)}) collective-permute-start(f32[6,192]{0,1:T(8,128)S(1)} %get-tuple-element.62), channel_id=1, source_target_pairs={{0,3},{1,4},{2,5},{3,6},{4,7},{8,11},{9,12},{10,13},{11,14},{12,15... | collective-permute-start | bytes 13832 | tf_op jit(solution)/shard_map/ppermute | solution.py:16
  283.1 84.8 %copy-start.9 = (s32[9216]{0:T(1024)S(1)}, s32[9216]{0:T(1024)}, u32[]{:S(2)}) copy-start(s32[9216]{0:T(1024)} %broadcast_clamp_fusion) | copy-start | bytes 110596
  345.6 130.1 %all-to-all-start.3 = ((f32[3,8,16]{2,0,1:T(4,128)}), f32[3,8,16]{2,0,1:T(4,128)}, u32[]{:S(2)}, u32[]{:S(2)}) async-start(f32[3,8,16]{2,0,1:T(4,128)} %copy.159), calls=%async_computation.3 | async-start | bytes 32768 | tf_op jit(solution)/shard_map/all_to_all | solution.py:99
  349.5 12.8 %collective-permute-start.13 = (f32[6,192]{0,1:T(8,128)S(1)}, f32[6,192]{0,1:T(8,128)S(1)}, u32[]{:S(2)}, u32[]{:S(2)}) collective-permute-start(f32[6,192]{0,1:T(8,128)S(1)} %get-tuple-element.61), channel_id=1, source_target_pairs={{3,0},{4,1},{5,2},{6,3},{7,4},{11,8},{12,9},{13,10},{14,11},{15,12... | collective-permute-start | bytes 13832 | tf_op jit(solution)/shard_map/ppermute | solution.py:16
  351.7 10.6 %collective-permute-start.14 = (f32[6,192]{0,1:T(8,128)S(1)}, f32[6,192]{0,1:T(8,128)S(1)}, u32[]{:S(2)}, u32[]{:S(2)}) collective-permute-start(f32[6,192]{0,1:T(8,128)S(1)} %get-tuple-element.60), channel_id=1, source_target_pairs={{0,4},{1,5},{2,6},{3,7},{8,12},{9,13},{10,14},{11,15},{16,20},{17,... | collective-permute-start | bytes 13832 | tf_op jit(solution)/shard_map/ppermute | solution.py:16
  358.0 9.9 %collective-permute-start.15 = (f32[6,192]{0,1:T(8,128)S(1)}, f32[6,192]{0,1:T(8,128)S(1)}, u32[]{:S(2)}, u32[]{:S(2)}) collective-permute-start(f32[6,192]{0,1:T(8,128)S(1)} %get-tuple-element.59), channel_id=1, source_target_pairs={{4,0},{5,1},{6,2},{7,3},{12,8},{13,9},{14,10},{15,11},{20,16},{21,... | collective-permute-start | bytes 13832 | tf_op jit(solution)/shard_map/ppermute | solution.py:16
  398.9 23.5 %copy-start.1 = (bf16[6,1,9216]{2,1,0:T(2,128)(2,1)S(1)}, bf16[6,1,9216]{2,1,0:T(2,128)(2,1)}, u32[]{:S(2)}) copy-start(bf16[6,1,9216]{2,1,0:T(2,128)(2,1)} %get-tuple-element.56) | copy-start | bytes 331780
  398.9 23.5 %copy-start.3 = (bf16[6,1,9216]{2,1,0:T(2,128)(2,1)S(1)}, bf16[6,1,9216]{2,1,0:T(2,128)(2,1)}, u32[]{:S(2)}) copy-start(bf16[6,1,9216]{2,1,0:T(2,128)(2,1)} %get-tuple-element.57) | copy-start | bytes 331780
  398.9 23.5 %copy-start.5 = (f32[6,1,9216]{2,1,0:T(1,128)S(1)}, f32[6,1,9216]{2,1,0:T(1,128)}, u32[]{:S(2)}) copy-start(f32[6,1,9216]{2,1,0:T(1,128)} %get-tuple-element.58) | copy-start | bytes 663556
  398.9 23.5 %copy-start.7 = (f32[9216]{0:T(1024)S(1)}, f32[9216]{0:T(1024)}, u32[]{:S(2)}) copy-start(f32[9216]{0:T(1024)} %fusion.38) | copy-start | bytes 110596
  422.8 53.7 %copy-start.41 = (f32[128]{0:T(128)S(1)}, f32[128]{0:T(128)}, u32[]{:S(2)}) copy-start(f32[128]{0:T(128)} %copy-done.40) | copy-start | bytes 1540
  422.8 53.7 %copy-start.33 = (f32[1,1,1,6,128]{4,1,3,2,0:T(1,128)S(1)}, f32[1,1,1,6,128]{4,1,3,2,0:T(1,128)}, u32[]{:S(2)}) copy-start(f32[1,1,1,6,128]{4,1,3,2,0:T(1,128)} %get-tuple-element.75) | copy-start | bytes 9220
  422.8 53.7 %copy-start.35 = (f32[1,1,1,6,128]{4,1,3,2,0:T(1,128)S(1)}, f32[1,1,1,6,128]{4,1,3,2,0:T(1,128)}, u32[]{:S(2)}) copy-start(f32[1,1,1,6,128]{4,1,3,2,0:T(1,128)} %get-tuple-element.76) | copy-start | bytes 9220
  422.8 53.7 %copy-start.37 = (f32[1,1,1,6,128]{4,1,3,2,0:T(1,128)S(1)}, f32[1,1,1,6,128]{4,1,3,2,0:T(1,128)}, u32[]{:S(2)}) copy-start(f32[1,1,1,6,128]{4,1,3,2,0:T(1,128)} %get-tuple-element.77) | copy-start | bytes 9220
  (7 other events, 26.4 us)
where the time goes:
time: 486 us; the launch traced here: 485 us
  local copies, waits for them, and re-layouts  160 us (33%)
  other arithmetic  127 us (26%)
  blocking collectives  121 us (25%)
  starting transfers between devices  63.6 us (13%)
  waiting for transfers between devices  11.5 us (2%)
    psum x2, blocking collectives, body(): load_total, column_disp = lax.psum((dense_loads, displaced), 'sec')  121 us
    scatter-add x2, other arithmetic, body(): jnp.zeros((NVAR, cells), jnp.float32).at[:, targets].add(contrib)  99.8 us
    gather x2, local copies, waits for them, and re-layouts, body(): gathered = extended[:, sources]  61.9 us
    slice x7, local copies, waits for them, and re-layouts, apply_blocks(): total = blocks[..., :, 0, :].astype(jnp.float32) * vector[..., 0:1, :]  52.2 us
    ppermute x16, starting transfers between devices, shifted(): lax.ppermute(value, axis, [(source, source + steps) for source in range(f...  48.6 us
    unnamed x119, local copies, waits for them, and re-layouts  14 us
    ppermute x16, waiting for transfers between devices, shifted(): lax.ppermute(value, axis, [(source, source + steps) for source in range(f...  11.5 us
  transfers between devices with their start and end apart: 20, of which 2 were waited for; matrix products, arithmetic and copies ran while one was open for 52% of the time, Pallas kernels for 0%

commit v1 on v0

--- a/solution.py
+++ b/solution.py
@@ -8,6 +8,22 @@
 NBR = 8
 ITERS = 2
 neighbour_offsets = (1, -1, 2, -2, 3, -3, 4, -4)
+
+
+def pairwise_exchange(x, axis, split, join):
+    ways, here = (lax.axis_size(axis), lax.axis_index(axis))
+    width = x.shape[split] // ways
+    lengths = list(x.shape)
+    lengths[split] = width
+    height = lengths[join]
+    lengths[join] = height * ways
+    full = jnp.zeros(lengths, x.dtype)
+    for mask in range(ways):
+        part = lax.dynamic_slice_in_dim(x, (here ^ mask) * width, width, axis=split)
+        if mask:
+            part = lax.ppermute(part, axis, [(d, d ^ mask) for d in range(ways)])
+        full = lax.dynamic_update_slice_in_dim(full, part, (here ^ mask) * height, axis=join)
+    return full
 
 
 def shifted(value, axis, steps):
@@ -95,10 +111,7 @@
         dense_loads = jnp.zeros((NLOAD, cells), jnp.float32).at[:, own_nodes].add(arrived)
         load_total, column_disp = lax.psum((dense_loads, displaced), "sec")
         looked_up = column_disp[:, own_nodes]
-        returned = (
-            lax.all_to_all(looked_up, "dom", split_axis=1, concat_axis=1, tiled=True)
-            * slot_mask[None, :]
-        )
+        returned = pairwise_exchange(looked_up, "dom", 1, 1) * slot_mask[None, :]
         pushed = apply_transposed(coupling_map, returned)
         flow_coupling = jnp.zeros((NVAR, cells), jnp.float32).at[:, surface_cells].add(pushed)
         struct_coupling = jnp.concatenate(

time: 486 us -> 508 us (1.045); the launches traced: 485 us -> 500 us
  waiting for transfers between devices: 11.5 us -> 21 us
    ppermute x0 -> x14, waiting for transfers between devices: none -> 13.5 us  [pairwise_exchange(): part = lax.ppermute(part, axis, [(d, d ^ mask) for d in range(ways)])]
    ppermute x0 -> x14, starting transfers between devices: none -> 13.2 us  [pairwise_exchange(): part = lax.ppermute(part, axis, [(d, d ^ mask) for d in range(ways)])]
    all_to_all x2 -> x0, starting transfers between devices: 7.75 us -> none  [body(): lax.all_to_all(looked_up, 'dom', split_axis=1, concat_axis=1, tiled=True)]
    unnamed x119 -> x121, local copies, waits for them, and re-layouts: 14 us -> 14.5 us
  transfers between devices with their start and end apart: 20 -> 32, of which waited for: 2 -> 12; matrix products, arithmetic and copies ran while one was open for 52% -> 10% of each run, Pallas kernels for 0% -> 0%
where the time goes in v1:
time: 508 us; the launch traced here: 500 us
  local copies, waits for them, and re-layouts  163 us (32%)
  other arithmetic  130 us (26%)
  blocking collectives  117 us (23%)
  starting transfers between devices  67 us (13%)
  waiting for transfers between devices  21 us (4%)
    psum x2, blocking collectives, body(): load_total, column_disp = lax.psum((dense_loads, displaced), 'sec')  117 us
    scatter-add x2, other arithmetic, body(): jnp.zeros((NVAR, cells), jnp.float32).at[:, targets].add(contrib)  100 us
    gather x2, local copies, waits for them, and re-layouts, body(): gathered = extended[:, sources]  61.9 us
    slice x7, local copies, waits for them, and re-layouts, apply_blocks(): total = blocks[..., :, 0, :].astype(jnp.float32) * vector[..., 0:1, :]  52.2 us
    ppermute x16, starting transfers between devices, shifted(): lax.ppermute(value, axis, [(source, source + steps) for source in range(f...  46.5 us
    unnamed x121, local copies, waits for them, and re-layouts  14.5 us
    ppermute x14, waiting for transfers between devices, pairwise_exchange(): part = lax.ppermute(part, axis, [(d, d ^ mask) for d in range(ways)])  13.5 us
    ppermute x14, starting transfers between devices, pairwise_exchange(): part = lax.ppermute(part, axis, [(d, d ^ mask) for d in range(ways)])  13.2 us
  transfers between devices with their start and end apart: 32, of which 12 were waited for; matrix products, arithmetic and copies ran while one was open for 10% of the time, Pallas kernels for 0%

profile of v1, /device:TPU:0, one launch (start us, length us, event | category | flops | bytes accessed | tf_op | source)
XLA Modules:
  0.0 499.7 jit_solution(16986496172776121617)
XLA Ops:
  0.0 1.1 copy.194
  1.8 2.6 gather_fusion
  4.4 0.9 fusion.57
  5.4 3.1 collective-permute-start
  8.5 1.3 collective-permute-start.1
  9.8 6.9 %collective-permute-start.2 = (f32[6,192]{0,1:T(8,128)}, f32[6,192]{0,1:T(8,128)}, u32[]{:S(2)}, u32[]{:S(2)}) collective-permute-start(f32[6,192]{0,1:T(8,128)} %get-tuple-element.72), channel_id=1, source_target_pairs={{0,2},{1,3},{2,4},{3,5},{4,6},{5,7},{8,10},{9,11},{10,12},{11,13},... | collective-permute-start | bytes 13832 | tf_op jit(solution)/shard_map/ppermute | solution.py:32
  20.5 3.9 all-to-all-start
  25.8 5.8 %fusion.55 = (bf16[6,1,9216]{2,1,0:T(2,128)(2,1)S(1)}, bf16[6,1,9216]{2,1,0:T(2,128)(2,1)S(1)}, bf16[6,1,9216]{2,1,0:T(2,128)(2,1)S(1)}, bf16[6,1,9216]{2,1,0:T(...) fusion(bf16[6,6,9216]{2,1,0:T(8,128)(2,1)} %bitcast.256), kind=kLoop, calls=%fused_computation.205 | loop fusion | flops 55296 | bytes 1437696 | tf_op jit(solution)/shard_map/slice | solution.py:41
  33.8 1.0 select_bitcast_fusion
  35.5 3.3 copy.191
  40.1 2.1 scatter_custom_fusion.1
  42.2 60.2 %all-reduce.3 = (f32[3,1536]{0,1:T(8,128)}, f32[3,1536]{0,1:T(8,128)}) all-reduce(f32[3,1536]{0,1:T(8,128)} %select_bitcast_fusion, f32[3,1536]{0,1:T(8,128)} %scatter_custom_fusion.1), channel_id=1, replica_groups=mesh['sec'=4,'dom'=8] {'sec'}, use_global_device_ids=true, to_apply=%region_3.4 | all-reduce | flops 9216 | bytes 73728 | tf_op jit(solution)/shard_map/psum | solution.py:112
  102.3 1.8 gather_fusion.3
  104.9 1.2 collective-permute-start.9
  107.4 1.4 collective-permute-done.9
  108.8 2.1 collective-permute-start.11
  112.0 1.5 collective-permute-done.11
  113.6 3.0 collective-permute-start.13
  117.2 2.0 collective-permute-done.13
  119.2 1.3 collective-permute-start.3
  120.8 1.1 collective-permute-done.14
  121.9 2.3 collective-permute-start.4
  125.3 2.0 scatter_custom_fusion.2
  127.3 1.3 collective-permute-start.5
  129.5 5.7 %collective-permute-start.6 = (f32[6,192]{0,1:T(8,128)S(1)}, f32[6,192]{0,1:T(8,128)S(1)}, u32[]{:S(2)}, u32[]{:S(2)}) collective-permute-start(f32[6,192]{0,1:T(8,128)S(1)} %copy-done.26), channel_id=1, source_target_pairs={{0,4},{1,5},{2,6},{3,7},{8,12},{9,13},{10,14},{11,15},{16,20},{17,... | collective-permute-start | bytes 13832 | tf_op jit(solution)/shard_map/ppermute | solution.py:32
  136.1 1.8 collective-permute-start.7
  140.7 3.3 collective-permute-done.7
  144.0 31.0 %gather_fusion.1 = f32[9216,6]{1,0:T(8,128)} fusion(f32[6,3072]{0,1:T(8,128)S(1)} %constant_dynamic-update-slice_fusion, s32[9216]{0:T(1024)S(1)} %copy-done.10), kind=kCustom, calls=%fused_computation.1 | custom fusion | bytes 479232 | tf_op jit(solution)/shard_map/gather | solution.py:105
  174.9 23.4 %slice_reduce_fusion.11 = (f32[9216]{0:T(1024)S(1)}, f32[9216]{0:T(1024)S(1)}, f32[9216]{0:T(1024)S(1)}, f32[9216]{0:T(1024)S(1)}, f32[9216]{0:T(1024)S(1)}, /*index=5*/f32[9216]{0:T(1024)S(1)}) fusion(f32[6,9216]{0,1:T(8,128)} %bitcast.245), kind=kLoop, calls=%fused_computation.25 | loop fusion | bytes 442368 | tf_op jit(solution)/shard_map/slice | solution.py:37
  198.8 2.9 copy.199
  201.8 50.1 %scatter_custom_fusion = f32[6,1536]{0,1:T(8,128)S(1)} fusion(s32[9216]{0:T(1024)} %bitcast.261, f32[9216,6]{1,0:T(8,128)} %copy.199, f32[]{:T(128)} %constant.16.clone.1), kind=kCustom, calls=%fused_computation.76 | custom fusion | flops 55296 | bytes 37376 | tf_op jit(solution)/shard_map/scatter-add | solution.py:107
  251.9 1.4 fusion.10
  253.3 2.3 slice_reduce_fusion.23
  255.7 2.6 constant_dynamic-update-slice_fusion.17
  258.3 4.9 gather_fusion.4
  263.2 2.1 slice_select_fusion
  265.3 1.9 gather_fusion.6
  268.6 3.3 all-to-all-start.1
  272.0 2.0 fusion.56
  274.0 2.9 collective-permute-start.15
  276.9 1.3 collective-permute-start.16
  278.2 5.8 %collective-permute-start.17 = (f32[6,192]{0,1:T(8,128)}, f32[6,192]{0,1:T(8,128)}, u32[]{:S(2)}, u32[]{:S(2)}) collective-permute-start(f32[6,192]{0,1:T(8,128)} %get-tuple-element.64), channel_id=1, source_target_pairs={{0,2},{1,3},{2,4},{3,5},{4,6},{5,7},{8,10},{9,11},{10,12},{11,13},... | collective-permute-start | bytes 13832 | tf_op jit(solution)/shard_map/ppermute | solution.py:32
  284.3 2.1 scatter_custom_fusion.4
  286.3 57.3 %all-reduce.2 = (f32[3,1536]{0,1:T(8,128)}, f32[3,1536]{0,1:T(8,128)}) all-reduce(f32[3,1536]{0,1:T(8,128)} %slice_select_fusion, f32[3,1536]{0,1:T(8,128)} %scatter_custom_fusion.4), channel_id=1, replica_groups=mesh['sec'=4,'dom'=8] {'sec'}, use_global_device_ids=true, to_apply=%region_8.9 | all-reduce | flops 9216 | bytes 73728 | tf_op jit(solution)/shard_map/psum | solution.py:112
  343.6 1.9 gather_fusion.7
  348.6 1.5 collective-permute-done.24
  350.2 1.1 collective-permute-start.26
  352.3 2.6 collective-permute-done.26
  355.9 1.5 collective-permute-start.29
  357.7 2.7 collective-permute-done.28
  360.4 1.3 collective-permute-start.18
  362.0 3.6 collective-permute-start.19
  366.6 2.0 scatter_custom_fusion.5
  368.7 1.3 collective-permute-start.20
  370.9 5.2 %collective-permute-start.21 = (f32[6,192]{0,1:T(8,128)S(1)}, f32[6,192]{0,1:T(8,128)S(1)}, u32[]{:S(2)}, u32[]{:S(2)}) collective-permute-start(f32[6,192]{0,1:T(8,128)S(1)} %get-tuple-element.60), channel_id=1, source_target_pairs={{0,4},{1,5},{2,6},{3,7},{8,12},{9,13},{10,14},{11,15},{16,20},{17,... | collective-permute-start | bytes 13832 | tf_op jit(solution)/shard_map/ppermute | solution.py:32
  377.0 1.5 collective-permute-start.22
  381.3 4.2 collective-permute-done.22
  385.5 31.0 %gather_fusion.5 = f32[9216,6]{1,0:T(8,128)} fusion(f32[6,3072]{0,1:T(8,128)S(1)} %constant_dynamic-update-slice_fusion.9, s32[9216]{0:T(1024)S(1)} %copy-done.11), kind=kCustom, calls=%fused_computation.5 | custom fusion | bytes 479232 | tf_op jit(solution)/shard_map/gather | solution.py:105
  416.4 23.4 %slice_reduce_fusion.5 = (f32[9216]{0:T(1024)S(1)}, f32[9216]{0:T(1024)S(1)}, f32[9216]{0:T(1024)S(1)}, f32[9216]{0:T(1024)S(1)}, f32[9216]{0:T(1024)S(1)}, /*index=5*/f32[9216]{0:T(1024)S(1)}) fusion(f32[6,9216]{0,1:T(8,128)} %bitcast.244), kind=kLoop, calls=%fused_computation.19 | loop fusion | bytes 442368 | tf_op jit(solution)/shard_map/slice | solution.py:37
  440.3 2.9 copy.215
  443.3 49.9 %scatter_custom_fusion.3 = f32[6,1536]{0,1:T(8,128)S(1)} fusion(s32[9216]{0:T(1024)} %bitcast.262, f32[9216,6]{1,0:T(8,128)} %copy.215, f32[]{:T(128)} %constant.16.clone.1), kind=kCustom, calls=%fused_computation.72 | custom fusion | flops 55296 | bytes 37376 | tf_op jit(solution)/shard_map/scatter-add | solution.py:107
  493.2 1.4 fusion.11
  494.6 2.3 slice_reduce_fusion.17
  497.0 1.7 fusion
  (249 shorter events, 33.6 us)
Async XLA Ops:
  0.0 16.6 %copy-start.34 = (f32[1,1,3,6,128]{4,1,3,2,0:T(1,128)S(1)}, f32[1,1,3,6,128]{4,1,3,2,0:T(1,128)}, u32[]{:S(2)}) copy-start(f32[1,1,3,6,128]{4,1,3,2,0:T(1,128)} %param.22) | copy-start | bytes 27652
  0.0 17.2 %copy-start.45 = (s32[1,1,128]{2,1,0:T(1,128)S(1)}, s32[1,1,128]{2,1,0:T(1,128)}, u32[]{:S(2)}) copy-start(s32[1,1,128]{2,1,0:T(1,128)} %param.20) | copy-start | bytes 1540
  0.0 19.8 %copy-start.46 = (s32[1,1,8]{2,1,0:T(1,128)S(1)}, s32[1,1,8]{2,1,0:T(1,128)}, u32[]{:S(2)}) copy-start(s32[1,1,8]{2,1,0:T(1,128)} %param.21) | copy-start | bytes 100
  5.4 19.7 %copy-start.32 = (s32[1,1,9216]{2,1,0:T(1,128)S(1)}, s32[1,1,9216]{2,1,0:T(1,128)}, u32[]{:S(2)}) copy-start(s32[1,1,9216]{2,1,0:T(1,128)} %param.16) | copy-start | bytes 110596
  5.4 121.9 %collective-permute-start = (f32[6,192]{0,1:T(8,128)}, f32[6,192]{0,1:T(8,128)}, u32[]{:S(2)}, u32[]{:S(2)}) collective-permute-start(f32[6,192]{0,1:T(8,128)} %get-tuple-element.74), channel_id=1, source_target_pairs={{0,1},{1,2},{2,3},{3,4},{4,5},{5,6},{6,7},{8,9},{9,10},{10,11},{11... | collective-permute-start | bytes 13832 | tf_op jit(solution)/shard_map/ppermute | solution.py:32
  8.5 121.0 %collective-permute-start.1 = (f32[6,192]{0,1:T(8,128)}, f32[6,192]{0,1:T(8,128)}, u32[]{:S(2)}, u32[]{:S(2)}) collective-permute-start(f32[6,192]{0,1:T(8,128)} %get-tuple-element.73), channel_id=1, source_target_pairs={{1,0},{2,1},{3,2},{4,3},{5,4},{6,5},{7,6},{9,8},{10,9},{11,10},{12... | collective-permute-start | bytes 13832 | tf_op jit(solution)/shard_map/ppermute | solution.py:32
  9.8 126.3 %collective-permute-start.2 = (f32[6,192]{0,1:T(8,128)}, f32[6,192]{0,1:T(8,128)}, u32[]{:S(2)}, u32[]{:S(2)}) collective-permute-start(f32[6,192]{0,1:T(8,128)} %get-tuple-element.72), channel_id=1, source_target_pairs={{0,2},{1,3},{2,4},{3,5},{4,6},{5,7},{8,10},{9,11},{10,12},{11,13},... | collective-permute-start | bytes 13832 | tf_op jit(solution)/shard_map/ppermute | solution.py:32
  17.9 16.9 %copy-start.44 = (s32[128]{0:T(128)}, s32[128]{0:T(128)S(1)}, u32[]{:S(2)}) copy-start(s32[128]{0:T(128)S(1)} %get-tuple-element.100) | copy-start | bytes 1540
  19.8 15.0 %copy-start.29 = (f32[8,16]{1,0:T(8,128)}, f32[8,16]{1,0:T(8,128)S(1)}, u32[]{:S(2)}) copy-start(f32[8,16]{1,0:T(8,128)S(1)} %fusion.50) | copy-start | bytes 1540
  20.5 18.7 %all-to-all-start = ((f32[3,8,16]{2,0,1:T(4,128)}), f32[3,8,16]{2,0,1:T(4,128)}, u32[]{:S(2)}, u32[]{:S(2)}) async-start(f32[3,8,16]{2,0,1:T(4,128)} %copy.200), calls=%async_computation | async-start | bytes 32768 | tf_op jit(solution)/shard_map/all_to_all | solution.py:109
  34.8 67.6 %copy-start.42 = (s32[1024]{0:T(1024)}, s32[1024]{0:T(1024)S(1)}, u32[]{:S(2)}) copy-start(s32[1024]{0:T(1024)S(1)} %pad_clamp_fusion.1) | copy-start | bytes 12292
  39.1 82.8 %copy-start.28 = (f32[6,192]{0,1:T(8,128)S(1)}, f32[6,192]{0,1:T(8,128)}, u32[]{:S(2)}) copy-start(f32[6,192]{0,1:T(8,128)} %get-tuple-element.70) | copy-start | bytes 13828
  39.1 86.0 %copy-start.35 = (f32[1,1,1,6,128]{4,1,3,2,0:T(1,128)S(1)}, f32[1,1,1,6,128]{4,1,3,2,0:T(1,128)}, u32[]{:S(2)}) copy-start(f32[1,1,1,6,128]{4,1,3,2,0:T(1,128)} %get-tuple-element.91) | copy-start | bytes 9220
  39.1 86.0 %copy-start.37 = (f32[1,1,1,6,128]{4,1,3,2,0:T(1,128)S(1)}, f32[1,1,1,6,128]{4,1,3,2,0:T(1,128)}, u32[]{:S(2)}) copy-start(f32[1,1,1,6,128]{4,1,3,2,0:T(1,128)} %get-tuple-element.92) | copy-start | bytes 9220
  39.1 86.0 %copy-start.39 = (f32[1,1,1,6,128]{4,1,3,2,0:T(1,128)S(1)}, f32[1,1,1,6,128]{4,1,3,2,0:T(1,128)}, u32[]{:S(2)}) copy-start(f32[1,1,1,6,128]{4,1,3,2,0:T(1,128)} %get-tuple-element.93) | copy-start | bytes 9220
  42.2 85.1 %copy-start.27 = (f32[6,192]{0,1:T(8,128)S(1)}, f32[6,192]{0,1:T(8,128)}, u32[]{:S(2)}) copy-start(f32[6,192]{0,1:T(8,128)} %get-tuple-element.69) | copy-start | bytes 13828
  42.2 87.3 %copy-start.26 = (f32[6,192]{0,1:T(8,128)S(1)}, f32[6,192]{0,1:T(8,128)}, u32[]{:S(2)}) copy-start(f32[6,192]{0,1:T(8,128)} %get-tuple-element.68) | copy-start | bytes 13828
  42.2 94.0 %copy-start.25 = (f32[6,192]{0,1:T(8,128)S(1)}, f32[6,192]{0,1:T(8,128)}, u32[]{:S(2)}) copy-start(f32[6,192]{0,1:T(8,128)} %get-tuple-element.67) | copy-start | bytes 13828
  102.3 41.6 %copy-start.10 = (s32[9216]{0:T(1024)S(1)}, s32[9216]{0:T(1024)}, u32[]{:S(2)}) copy-start(s32[9216]{0:T(1024)} %broadcast_clamp_fusion) | copy-start | bytes 110596
  104.9 1.4 collective-permute-start.8
  104.9 3.9 collective-permute-start.9
  106.2 4.9 collective-permute-start.10
  108.8 4.8 collective-permute-start.11
  111.1 5.7 %collective-permute-start.12 = (f32[3,16]{0,1:T(8,128)}, f32[3,16]{0,1:T(8,128)S(1)}, u32[]{:S(2)}, u32[]{:S(2)}) collective-permute-start(f32[3,16]{0,1:T(8,128)} %get-tuple-element.85), channel_id=1, source_target_pairs={{0,5},{1,4},{2,7},{3,6},{4,1},{5,0},{6,3},{7,2},{8,13},{9,12},{10,... | collective-permute-start | bytes 584 | tf_op jit(solution)/shard_map/ppermute | solution.py:24
  113.6 5.7 %collective-permute-start.13 = (f32[3,16]{0,1:T(8,128)}, f32[3,16]{0,1:T(8,128)S(1)}, u32[]{:S(2)}, u32[]{:S(2)}) collective-permute-start(f32[3,16]{0,1:T(8,128)} %get-tuple-element.84), channel_id=1, source_target_pairs={{0,6},{1,7},{2,4},{3,5},{4,2},{5,3},{6,0},{7,1},{8,14},{9,15},{10,... | collective-permute-start | bytes 584 | tf_op jit(solution)/shard_map/ppermute | solution.py:24
  116.9 5.0 %collective-permute-start.14 = (f32[3,16]{0,1:T(8,128)S(1)}, f32[3,16]{0,1:T(8,128)S(1)}, u32[]{:S(2)}, u32[]{:S(2)}) collective-permute-start(f32[3,16]{0,1:T(8,128)S(1)} %get-tuple-element.83), channel_id=1, source_target_pairs={{0,7},{1,6},{2,5},{3,4},{4,3},{5,2},{6,1},{7,0},{8,15},{9,14},{10,... | collective-permute-start | bytes 584 | tf_op jit(solution)/shard_map/ppermute | solution.py:24
  119.2 19.6 %collective-permute-start.3 = (f32[6,192]{0,1:T(8,128)}, f32[6,192]{0,1:T(8,128)}, u32[]{:S(2)}, u32[]{:S(2)}) collective-permute-start(f32[6,192]{0,1:T(8,128)} %get-tuple-element.71), channel_id=1, source_target_pairs={{2,0},{3,1},{4,2},{5,3},{6,4},{7,5},{10,8},{11,9},{12,10},{13,11},... | collective-permute-start | bytes 13832 | tf_op jit(solution)/shard_map/ppermute | solution.py:32
  121.9 17.8 %collective-permute-start.4 = (f32[6,192]{0,1:T(8,128)S(1)}, f32[6,192]{0,1:T(8,128)}, u32[]{:S(2)}, u32[]{:S(2)}) collective-permute-start(f32[6,192]{0,1:T(8,128)S(1)} %copy-done.28), channel_id=1, source_target_pairs={{0,3},{1,4},{2,5},{3,6},{4,7},{8,11},{9,12},{10,13},{11,14},{12,15... | collective-permute-start | bytes 13832 | tf_op jit(solution)/shard_map/ppermute | solution.py:32
  127.3 13.3 %collective-permute-start.5 = (f32[6,192]{0,1:T(8,128)S(1)}, f32[6,192]{0,1:T(8,128)S(1)}, u32[]{:S(2)}, u32[]{:S(2)}) collective-permute-start(f32[6,192]{0,1:T(8,128)S(1)} %copy-done.27), channel_id=1, source_target_pairs={{3,0},{4,1},{5,2},{6,3},{7,4},{11,8},{12,9},{13,10},{14,11},{15,12... | collective-permute-start | bytes 13832 | tf_op jit(solution)/shard_map/ppermute | solution.py:32
  129.5 11.2 %collective-permute-start.6 = (f32[6,192]{0,1:T(8,128)S(1)}, f32[6,192]{0,1:T(8,128)S(1)}, u32[]{:S(2)}, u32[]{:S(2)}) collective-permute-start(f32[6,192]{0,1:T(8,128)S(1)} %copy-done.26), channel_id=1, source_target_pairs={{0,4},{1,5},{2,6},{3,7},{8,12},{9,13},{10,14},{11,15},{16,20},{17,... | collective-permute-start | bytes 13832 | tf_op jit(solution)/shard_map/ppermute | solution.py:32
  136.1 7.8 %collective-permute-start.7 = (f32[6,192]{0,1:T(8,128)S(1)}, f32[6,192]{0,1:T(8,128)S(1)}, u32[]{:S(2)}, u32[]{:S(2)}) collective-permute-start(f32[6,192]{0,1:T(8,128)S(1)} %copy-done.25), channel_id=1, source_target_pairs={{4,0},{5,1},{6,2},{7,3},{12,8},{13,9},{14,10},{15,11},{20,16},{21,... | collective-permute-start | bytes 13832 | tf_op jit(solution)/shard_map/ppermute | solution.py:32
  174.9 23.5 %copy-start.2 = (bf16[6,1,9216]{2,1,0:T(2,128)(2,1)S(1)}, bf16[6,1,9216]{2,1,0:T(2,128)(2,1)}, u32[]{:S(2)}) copy-start(bf16[6,1,9216]{2,1,0:T(2,128)(2,1)} %get-tuple-element.56) | copy-start | bytes 331780
  174.9 23.5 %copy-start.4 = (bf16[6,1,9216]{2,1,0:T(2,128)(2,1)S(1)}, bf16[6,1,9216]{2,1,0:T(2,128)(2,1)}, u32[]{:S(2)}) copy-start(bf16[6,1,9216]{2,1,0:T(2,128)(2,1)} %get-tuple-element.57) | copy-start | bytes 331780
  174.9 23.5 %copy-start.6 = (f32[6,1,9216]{2,1,0:T(1,128)S(1)}, f32[6,1,9216]{2,1,0:T(1,128)}, u32[]{:S(2)}) copy-start(f32[6,1,9216]{2,1,0:T(1,128)} %get-tuple-element.58) | copy-start | bytes 663556
  174.9 23.5 %copy-start.8 = (f32[9216]{0:T(1024)S(1)}, f32[9216]{0:T(1024)}, u32[]{:S(2)}) copy-start(f32[9216]{0:T(1024)} %fusion.38) | copy-start | bytes 110596
  198.8 53.0 %copy-start.1 = (f32[6,1536]{0,1:T(8,128)S(1)}, f32[6,1536]{0,1:T(8,128)}, u32[]{:S(2)}) copy-start(f32[6,1536]{0,1:T(8,128)} %scatter_custom_fusion.2) | copy-start | bytes 110596
  198.8 56.8 %slice-start = ((s8[4718592]{0:T(1024)(128)(4,1)}), s8[524288]{0:T(1024)(128)(4,1)S(1)}, s32[]{:S(2)}) async-start(s8[4718592]{0:T(1024)(128)(4,1)} %bitcast.246), calls=%async_computation.2 | async-start | bytes 1048576
  258.3 9.7 %copy-start.22 = (f32[3,8,16]{2,1,0:T(8,128)S(1)}, f32[3,8,16]{2,1,0:T(8,128)}, u32[]{:S(2)}) copy-start(f32[3,8,16]{2,1,0:T(8,128)} %copy-done.21) | copy-start | bytes 4612
  268.6 15.4 %all-to-all-start.1 = ((f32[3,8,16]{2,0,1:T(4,128)}), f32[3,8,16]{2,0,1:T(4,128)S(1)}, u32[]{:S(2)}, u32[]{:S(2)}) async-start(f32[3,8,16]{2,0,1:T(4,128)} %copy.216), calls=%async_computation.1 | async-start | bytes 32768 | tf_op jit(solution)/shard_map/all_to_all | solution.py:109
  274.0 92.5 %copy-start.36 = (f32[1,1,1,6,128]{4,1,3,2,0:T(1,128)S(1)}, f32[1,1,1,6,128]{4,1,3,2,0:T(1,128)}, u32[]{:S(2)}) copy-start(f32[1,1,1,6,128]{4,1,3,2,0:T(1,128)} %get-tuple-element.91) | copy-start | bytes 9220
  274.0 92.5 %copy-start.38 = (f32[1,1,1,6,128]{4,1,3,2,0:T(1,128)S(1)}, f32[1,1,1,6,128]{4,1,3,2,0:T(1,128)}, u32[]{:S(2)}) copy-start(f32[1,1,1,6,128]{4,1,3,2,0:T(1,128)} %get-tuple-element.92) | copy-start | bytes 9220
  274.0 92.5 %copy-start.40 = (f32[1,1,1,6,128]{4,1,3,2,0:T(1,128)S(1)}, f32[1,1,1,6,128]{4,1,3,2,0:T(1,128)}, u32[]{:S(2)}) copy-start(f32[1,1,1,6,128]{4,1,3,2,0:T(1,128)} %get-tuple-element.93) | copy-start | bytes 9220
  274.0 94.7 %collective-permute-start.15 = (f32[6,192]{0,1:T(8,128)}, f32[6,192]{0,1:T(8,128)}, u32[]{:S(2)}, u32[]{:S(2)}) collective-permute-start(f32[6,192]{0,1:T(8,128)} %get-tuple-element.66), channel_id=1, source_target_pairs={{0,1},{1,2},{2,3},{3,4},{4,5},{5,6},{6,7},{8,9},{9,10},{10,11},{11... | collective-permute-start | bytes 13832 | tf_op jit(solution)/shard_map/ppermute | solution.py:32
  276.9 93.9 %collective-permute-start.16 = (f32[6,192]{0,1:T(8,128)}, f32[6,192]{0,1:T(8,128)}, u32[]{:S(2)}, u32[]{:S(2)}) collective-permute-start(f32[6,192]{0,1:T(8,128)} %get-tuple-element.65), channel_id=1, source_target_pairs={{1,0},{2,1},{3,2},{4,3},{5,4},{6,5},{7,6},{9,8},{10,9},{11,10},{12... | collective-permute-start | bytes 13832 | tf_op jit(solution)/shard_map/ppermute | solution.py:32
  278.2 98.8 %collective-permute-start.17 = (f32[6,192]{0,1:T(8,128)}, f32[6,192]{0,1:T(8,128)}, u32[]{:S(2)}, u32[]{:S(2)}) collective-permute-start(f32[6,192]{0,1:T(8,128)} %get-tuple-element.64), channel_id=1, source_target_pairs={{0,2},{1,3},{2,4},{3,5},{4,6},{5,7},{8,10},{9,11},{10,12},{11,13},... | collective-permute-start | bytes 13832 | tf_op jit(solution)/shard_map/ppermute | solution.py:32
  343.6 41.8 %copy-start.11 = (s32[9216]{0:T(1024)S(1)}, s32[9216]{0:T(1024)}, u32[]{:S(2)}) copy-start(s32[9216]{0:T(1024)} %broadcast_clamp_fusion) | copy-start | bytes 110596
  346.2 1.4 collective-permute-start.23
  346.3 3.9 collective-permute-start.24
  347.6 3.9 collective-permute-start.25
  350.2 4.8 collective-permute-start.26
  351.5 4.3 collective-permute-start.27
  354.9 5.4 %collective-permute-start.28 = (f32[3,16]{0,1:T(8,128)S(1)}, f32[3,16]{0,1:T(8,128)S(1)}, u32[]{:S(2)}, u32[]{:S(2)}) collective-permute-start(f32[3,16]{0,1:T(8,128)S(1)} %get-tuple-element.76), channel_id=1, source_target_pairs={{0,6},{1,7},{2,4},{3,5},{4,2},{5,3},{6,0},{7,1},{8,14},{9,15},{10,... | collective-permute-start | bytes 584 | tf_op jit(solution)/shard_map/ppermute | solution.py:24
  355.9 6.1 %collective-permute-start.29 = (f32[3,16]{0,1:T(8,128)S(1)}, f32[3,16]{0,1:T(8,128)S(1)}, u32[]{:S(2)}, u32[]{:S(2)}) collective-permute-start(f32[3,16]{0,1:T(8,128)S(1)} %get-tuple-element.75), channel_id=1, source_target_pairs={{0,7},{1,6},{2,5},{3,4},{4,3},{5,2},{6,1},{7,0},{8,15},{9,14},{10,... | collective-permute-start | bytes 584 | tf_op jit(solution)/shard_map/ppermute | solution.py:24
  360.4 19.0 %collective-permute-start.18 = (f32[6,192]{0,1:T(8,128)}, f32[6,192]{0,1:T(8,128)}, u32[]{:S(2)}, u32[]{:S(2)}) collective-permute-start(f32[6,192]{0,1:T(8,128)} %get-tuple-element.63), channel_id=1, source_target_pairs={{2,0},{3,1},{4,2},{5,3},{6,4},{7,5},{10,8},{11,9},{12,10},{13,11},... | collective-permute-start | bytes 13832 | tf_op jit(solution)/shard_map/ppermute | solution.py:32
  362.0 18.3 %collective-permute-start.19 = (f32[6,192]{0,1:T(8,128)S(1)}, f32[6,192]{0,1:T(8,128)}, u32[]{:S(2)}, u32[]{:S(2)}) collective-permute-start(f32[6,192]{0,1:T(8,128)S(1)} %get-tuple-element.62), channel_id=1, source_target_pairs={{0,3},{1,4},{2,5},{3,6},{4,7},{8,11},{9,12},{10,13},{11,14},{12,15... | collective-permute-start | bytes 13832 | tf_op jit(solution)/shard_map/ppermute | solution.py:32
  368.7 12.5 %collective-permute-start.20 = (f32[6,192]{0,1:T(8,128)S(1)}, f32[6,192]{0,1:T(8,128)S(1)}, u32[]{:S(2)}, u32[]{:S(2)}) collective-permute-start(f32[6,192]{0,1:T(8,128)S(1)} %get-tuple-element.61), channel_id=1, source_target_pairs={{3,0},{4,1},{5,2},{6,3},{7,4},{11,8},{12,9},{13,10},{14,11},{15,12... | collective-permute-start | bytes 13832 | tf_op jit(solution)/shard_map/ppermute | solution.py:32
  370.9 10.4 %collective-permute-start.21 = (f32[6,192]{0,1:T(8,128)S(1)}, f32[6,192]{0,1:T(8,128)S(1)}, u32[]{:S(2)}, u32[]{:S(2)}) collective-permute-start(f32[6,192]{0,1:T(8,128)S(1)} %get-tuple-element.60), channel_id=1, source_target_pairs={{0,4},{1,5},{2,6},{3,7},{8,12},{9,13},{10,14},{11,15},{16,20},{17,... | collective-permute-start | bytes 13832 | tf_op jit(solution)/shard_map/ppermute | solution.py:32
  377.0 8.5 %collective-permute-start.22 = (f32[6,192]{0,1:T(8,128)S(1)}, f32[6,192]{0,1:T(8,128)S(1)}, u32[]{:S(2)}, u32[]{:S(2)}) collective-permute-start(f32[6,192]{0,1:T(8,128)S(1)} %get-tuple-element.59), channel_id=1, source_target_pairs={{4,0},{5,1},{6,2},{7,3},{12,8},{13,9},{14,10},{15,11},{20,16},{21,... | collective-permute-start | bytes 13832 | tf_op jit(solution)/shard_map/ppermute | solution.py:32
  416.4 23.5 %copy-start.3 = (bf16[6,1,9216]{2,1,0:T(2,128)(2,1)S(1)}, bf16[6,1,9216]{2,1,0:T(2,128)(2,1)}, u32[]{:S(2)}) copy-start(bf16[6,1,9216]{2,1,0:T(2,128)(2,1)} %get-tuple-element.56) | copy-start | bytes 331780
  416.4 23.5 %copy-start.5 = (bf16[6,1,9216]{2,1,0:T(2,128)(2,1)S(1)}, bf16[6,1,9216]{2,1,0:T(2,128)(2,1)}, u32[]{:S(2)}) copy-start(bf16[6,1,9216]{2,1,0:T(2,128)(2,1)} %get-tuple-element.57) | copy-start | bytes 331780
  416.4 23.5 %copy-start.7 = (f32[6,1,9216]{2,1,0:T(1,128)S(1)}, f32[6,1,9216]{2,1,0:T(1,128)}, u32[]{:S(2)}) copy-start(f32[6,1,9216]{2,1,0:T(1,128)} %get-tuple-element.58) | copy-start | bytes 663556
  416.4 23.5 %copy-start.9 = (f32[9216]{0:T(1024)S(1)}, f32[9216]{0:T(1024)}, u32[]{:S(2)}) copy-start(f32[9216]{0:T(1024)} %fusion.38) | copy-start | bytes 110596
  440.3 52.9 %copy-start = (f32[6,1536]{0,1:T(8,128)S(1)}, f32[6,1536]{0,1:T(8,128)}, u32[]{:S(2)}) copy-start(f32[6,1536]{0,1:T(8,128)} %scatter_custom_fusion.5) | copy-start | bytes 110596
  440.3 56.6 %slice-start.2 = ((s8[4718592]{0:T(1024)(128)(4,1)}), s8[524288]{0:T(1024)(128)(4,1)S(1)}, s32[]{:S(2)}) async-start(s8[4718592]{0:T(1024)(128)(4,1)} %bitcast.249), calls=%async_computation.4 | async-start | bytes 1048576
  (20 other events, 151.1 us)
